TPU v7x, 256 devices: a whole 4x4x8 slice. The times are simulated.
256 devices in a mesh: dp: 8 (over y, core), cent: 32 (over x, z).
Axes of the slice: x: 4, y: 4, z: 8, core: 2. Of those that a mesh axis runs over, the one named last changes fastest.
Arguments:
- passages: bfloat16 [32768, 768], P(('dp', 'cent')), may hold values from -10 to 10
- queries: bfloat16 [1024, 768], P(('dp', 'cent')), may hold values from -10 to 10
- init_centroids: float32 [8192, 768], P('cent'), may hold values from -12 to 12
- pattern: int32 [1024, 4], replicated, may hold values from 0 to 255, all different within a row
- positive_offset: int32 [1024], replicated, may hold values from 0 to 127
Outputs:
- centroids: float32 [8192, 768], P('cent')
- loss: float32 [1024], P(('dp', 'cent'))
Inputs may be any that keep to these rules, and one draw needn't show every extreme that they name: `pattern`: each row names 4 different blocks.
All inputs are finite; a program needn't handle non-finite values.
Results may differ from a plain program's by a relative error of at most 0.0055.
Values may be sent and summed in bfloat16 or wider, within the bound.
A program may use at most 64 MiB of HBM per device.

v0:
```python
import jax
import jax.numpy as jnp
from jax import lax
from jax.sharding import PartitionSpec as P

BLOCK = 128
ITERS = 2
sharpness = 0.05
sharpening_factor = 0.05
prior_weight = 1.0


def merged(value, axis, join):
    pieces = jax.tree.map(lambda part: lax.all_gather(part, axis), value)
    head = jax.tree.map(lambda part: part[0], pieces)
    tail = jax.tree.map(lambda part: part[1:], pieces)
    so_far, _ = lax.scan(lambda so_far, section: (join(so_far, section), None), head, tail)
    return so_far


def combine_query(first, second):
    upper = jnp.maximum(first[0], second[0])
    total = first[1] * jnp.exp(first[0] - upper) + second[1] * jnp.exp(second[0] - upper)
    return (upper, total, first[2] + second[2])


def on_device(passages, queries, init_centroids, pattern, positive_offset):
    gathered = lax.all_gather(passages, "cent", axis=0, tiled=True)
    cluster_means = init_centroids
    for step_index in range(ITERS):
        centers_half = cluster_means.astype(jnp.bfloat16)
        cluster_center_norms = jnp.sum(cluster_means * cluster_means, axis=1)
        unnormalized_log_odds = sharpness * (
            2.0 * jnp.dot(gathered, centers_half.T, preferred_element_type=jnp.float32)
            - cluster_center_norms[None, :]
        )
        row_max = lax.pmax(jnp.max(unnormalized_log_odds, axis=1), "cent")
        weights_exp = jnp.exp(unnormalized_log_odds - row_max[:, None])
        row_total = lax.psum(jnp.sum(weights_exp, axis=1), "cent")
        resp = weights_exp / row_total[:, None]
        numer = lax.dot_general(
            resp.astype(jnp.bfloat16),
            gathered,
            (((0,), (0,)), ((), ())),
            preferred_element_type=jnp.float32,
        )
        counts = jnp.sum(resp, axis=0)
        numer, counts = lax.psum((numer, counts), "dp")
        cluster_means = (numer + prior_weight * cluster_means) / (counts[:, None] + prior_weight)
    query_collection = lax.all_gather(queries, ("dp", "cent"), axis=0, tiled=True)
    local_rows = passages.shape[0]
    linear = lax.axis_index(("dp", "cent"))
    first_row = linear * local_rows
    local_blocks = first_row // BLOCK + jnp.arange(local_rows // BLOCK, dtype=jnp.int32)
    paired_entries = jnp.any(pattern[:, :, None] == local_blocks[None, None, :], axis=1)
    allowed = jnp.repeat(paired_entries, BLOCK, axis=1)
    affinity_matrix = (
        jnp.dot(query_collection, passages.T, preferred_element_type=jnp.float32)
        * sharpening_factor
    )
    target_col = pattern[:, 0] * BLOCK + positive_offset - first_row
    columns = jnp.arange(local_rows, dtype=jnp.int32)
    positive = jnp.sum(
        jnp.where(columns[None, :] == target_col[:, None], affinity_matrix, 0.0), axis=1
    )
    local_max = jnp.max(jnp.where(allowed, affinity_matrix, -1e30), axis=1)
    local_total = jnp.sum(
        jnp.where(allowed, jnp.exp(affinity_matrix - local_max[:, None]), 0.0), axis=1
    )
    query_max, query_total, positive_all = merged(
        (local_max, local_total, positive), ("dp", "cent"), combine_query
    )
    whole_loss = jnp.log(query_total) + query_max - positive_all
    own_count = queries.shape[0]
    own_loss = lax.dynamic_slice_in_dim(whole_loss, linear * own_count, own_count, 0)
    return (cluster_means, own_loss)


def solution(mesh):
    placed = (P(("dp", "cent"), None), P(("dp", "cent"), None), P("cent", None), P(), P())
    return jax.shard_map(
        on_device,
        mesh=mesh,
        in_specs=placed,
        out_specs=(P("cent", None), P(("dp", "cent"))),
        check_vma=False,
    )
```

profile of v0, /device:TPU:2, one launch (start us, length us, event | category | flops | bytes accessed | tf_op | source)
XLA Modules:
  0.0 1376.9 jit_solution(4740807136776224495)
XLA Ops:
  8.7 108.5 %all-gather.18.cloned.1.call-done = bf16[256,4,768]{2,1,0:T(4,128)(2,1)} async-done(((bf16[1,4,768]{2,1,0:T(4,128)(2,1)}), bf16[256,4,768]{2,1,0:T(4,128)(2,1)}) %all-gather.18.cloned.1.call-update) | async-done | bytes 1572880 | tf_op jit(solution)/shard_map/all_gather | solution.py:50
  117.2 2.7 reshape.42
  120.0 2.2 select_reduce_fusion.2
  125.8 97.7 %all-gather.12.cloned.1.call-done = f32[262144]{0:T(1024)} async-done(((f32[1024]{0:T(1024)}), f32[262144]{0:T(1024)}) %all-gather.12.cloned.1.call-update) | async-done | bytes 1048592 | tf_op jit(solution)/shard_map/all_gather | solution.py:14
  224.9 103.3 %all-gather.14.cloned.1.call-done = f32[262144]{0:T(1024)} async-done(((f32[1024]{0:T(1024)}), f32[262144]{0:T(1024)}) %all-gather.14.cloned.1.call-update) | async-done | bytes 1048592 | tf_op jit(solution)/shard_map/all_gather | solution.py:14
  330.6 102.2 %all-gather.16.cloned.1.call-done = f32[262144]{0:T(1024)} async-done(((f32[1024]{0:T(1024)}), f32[262144]{0:T(1024)}) %all-gather.16.cloned.1.call-update) | async-done | bytes 1048592 | tf_op jit(solution)/shard_map/all_gather | solution.py:14
  435.2 218.6 %while.14 = (s32[]{:T(128)}, f32[1024]{0:T(1024)S(1)}, f32[1024]{0:T(1024)S(1)}, f32[1024]{0:T(1024)S(1)}, f32[255,1024]{1,0:T(8,128)S(1)}, /*index=5*/f32[255,1024]{1,0:T(8,128)}, f32[255,1024]{1,0:T(8,128)}, s32[]{:T(128)}) while((s32[]{:T(128)}, f32[1024]{0:T(1024)S(1)}, f32[1024]{0:T(1024)S(1)}, f32[1024]{0:T(1024)S(1)}, ...), condition=%wide.region_21.22_spmd, body=%wide.region_20.21_spmd.sunk | while | flops 7170 | bytes 61541 | solution.py:17
  654.5 6.7 fusion.18
  661.1 130.3 %pmax.14 = f32[4096]{0:T(1024)S(1)} all-reduce(f32[4096]{0:T(1024)S(1)} %get-tuple-element.66), channel_id=1, replica_groups=mesh['dp'=8,'cent'=32] {'cent'}, use_global_device_ids=true, to_apply=%region_2.0 | all-reduce | flops 4096 | bytes 32768 | tf_op jit(solution)/shard_map/pmax | solution.py:37
  791.4 2.8 fusion.5
  794.2 137.7 %psum.42 = f32[4096]{0:T(1024)S(1)} all-reduce(f32[4096]{0:T(1024)S(1)} %fusion.5), channel_id=1, replica_groups=mesh['dp'=8,'cent'=32] {'cent'}, use_global_device_ids=true, to_apply=%region_4.0 | all-reduce | flops 4096 | bytes 32768 | tf_op jit(solution)/shard_map/psum | solution.py:39
  931.8 6.8 fusion.10
  938.7 3.0 fusion.14
  941.7 12.4 psum.44
  954.1 57.1 %all-reduce.3.cloned.1.call-done = f32[256,768]{1,0:T(8,128)} async-done(((f32[256,768]{1,0:T(8,128)}), f32[256,768]{1,0:T(8,128)}) %all-reduce.3.cloned.1.call-update) | async-done | bytes 786448 | tf_op jit(solution)/shard_map/psum | solution.py:48
  1012.6 6.7 fusion.19
  1019.3 131.0 %pmax.15 = f32[4096]{0:T(1024)S(1)} all-reduce(f32[4096]{0:T(1024)S(1)} %get-tuple-element.68), channel_id=1, replica_groups=mesh['dp'=8,'cent'=32] {'cent'}, use_global_device_ids=true, to_apply=%region_10.0 | all-reduce | flops 4096 | bytes 32768 | tf_op jit(solution)/shard_map/pmax | solution.py:37
  1150.3 2.8 fusion.6
  1153.1 137.9 %psum.45 = f32[4096]{0:T(1024)S(1)} all-reduce(f32[4096]{0:T(1024)S(1)} %fusion.6), channel_id=1, replica_groups=mesh['dp'=8,'cent'=32] {'cent'}, use_global_device_ids=true, to_apply=%region_12.0 | all-reduce | flops 4096 | bytes 32768 | tf_op jit(solution)/shard_map/psum | solution.py:39
  1291.0 6.8 fusion.8
  1297.8 3.0 fusion.12
  1300.8 12.4 psum.47
  1313.2 54.7 %all-reduce.5.cloned.1.call-done = f32[256,768]{1,0:T(8,128)} async-done(((f32[256,768]{1,0:T(8,128)}), f32[256,768]{1,0:T(8,128)}) %all-reduce.5.cloned.1.call-update) | async-done | bytes 786448 | tf_op jit(solution)/shard_map/psum | solution.py:48
  1367.9 2.1 add_divide_fusion
  (1061 shorter events, 222.1 us)
Async XLA Ops:
  7.2 115.8 %copy-start.1 = (s32[1024]{0:T(1024)S(1)}, s32[1024]{0:T(1024)}, u32[]{:S(2)}) copy-start(s32[1024]{0:T(1024)} %param.11) | copy-start | bytes 12292
  7.2 118.5 %copy-start = (f32[256,768]{1,0:T(8,128)S(1)}, f32[256,768]{1,0:T(8,128)}, u32[]{:S(2)}) copy-start(f32[256,768]{1,0:T(8,128)} %param.9) | copy-start | bytes 2359300
  7.2 110.0 %all-gather.18.cloned.1.call-start = ((), (), s32[]{:S(2)}) async-start(), calls=%async_computation.6 | async-start | bytes 1579008 | tf_op jit(solution)/shard_map/all_gather | solution.py:50
  7.9 215.5 %all-gather.12.cloned.1.call-start = ((), (), s32[]{:S(2)}) async-start(), calls=%async_computation.3 | async-start | bytes 1052672 | tf_op jit(solution)/shard_map/all_gather | solution.py:14
  122.2 206.0 %all-gather.14.cloned.1.call-start = ((), (), s32[]{:S(2)}) async-start(), calls=%async_computation.4 | async-start | bytes 1052672 | tf_op jit(solution)/shard_map/all_gather | solution.py:14
  124.4 308.4 %all-gather.16.cloned.1.call-start = ((), (), s32[]{:S(2)}) async-start(), calls=%async_computation.5 | async-start | bytes 1052672 | tf_op jit(solution)/shard_map/all_gather | solution.py:14
  125.0 529.4 %all-gather.10.cloned.1.call-start = ((), (), s32[]{:S(2)}) async-start(), calls=%async_computation | async-start | bytes 6488064 | tf_op jit(solution)/shard_map/all_gather | solution.py:28
  125.6 885.7 %all-reduce.3.cloned.1.call-start = ((), (), s32[]{:S(2)}) async-start(), calls=%async_computation.1 | async-start | bytes 1572864 | tf_op jit(solution)/shard_map/psum | solution.py:48
  224.9 210.3 %slice-start = ((f32[262144]{0:T(1024)}), f32[1024]{0:T(1024)S(1)}, s32[]{:S(2)}) async-start(f32[262144]{0:T(1024)} %all-gather.12.cloned.1.call-done), calls=%async_computation.7 | async-start | bytes 8192 | tf_op jit(solution)/shard_map/slice | solution.py:15
  328.2 107.0 %slice-start.1 = ((f32[262144]{0:T(1024)}), f32[1024]{0:T(1024)S(1)}, s32[]{:S(2)}) async-start(f32[262144]{0:T(1024)} %all-gather.14.cloned.1.call-done), calls=%async_computation.8 | async-start | bytes 8192 | tf_op jit(solution)/shard_map/slice | solution.py:15
  432.8 2.4 slice-start.2
  938.7 429.2 %all-reduce.5.cloned.1.call-start = ((), (), s32[]{:S(2)}) async-start(), calls=%async_computation.2 | async-start | bytes 1572864 | tf_op jit(solution)/shard_map/psum | solution.py:48
Sparse Core Ops, SparseCore 0:
  11.6 105.6 all-gather.17
  122.3 101.0 all-gather.11
  227.2 100.9 all-gather.13
  331.8 100.9 all-gather.15
  435.2 86.4 all-gather.9
  938.8 72.4 all-reduce.2
  1297.9 69.9 all-reduce.4
where the time goes:
time: 1400 us; the launch traced here: 1380 us
  blocking collectives  562 us (40%)
  waiting for transfers between devices  525 us (38%)
  local copies, waits for them, and re-layouts  214 us (15%)
  matrix products  29.1 us (2%)
  other arithmetic  22.3 us (2%)
  between operations  14.2 us (1%)
    all_gather x3, waiting for transfers between devices, merged(): pieces = jax.tree.map(lambda part: lax.all_gather(part, axis), value)  303 us
    psum x2, blocking collectives, on_device(): row_total = lax.psum(jnp.sum(weights_exp, axis=1), 'cent')  276 us
    pmax x2, blocking collectives, on_device(): row_max = lax.pmax(jnp.max(unnormalized_log_odds, axis=1), 'cent')  261 us
    dynamic_slice x510, local copies, waits for them, and re-layouts, merged(): lax.scan(lambda so_far, section: (join(so_far, section), None), head, tail)  205 us
    psum x2, waiting for transfers between devices, on_device(): numer, counts = lax.psum((numer, counts), 'dp')  112 us
    all_gather x1, waiting for transfers between devices, on_device(): lax.all_gather(queries, ('dp', 'cent'), axis=0, tiled=True)  109 us
  transfers between devices with their start and end apart: 7, of which 6 were waited for; matrix products, arithmetic and copies ran while one was open for 16% of the time, Pallas kernels for 0%

commit v1 on v0

--- a/solution.py
+++ b/solution.py
@@ -36,7 +36,7 @@
         )
         row_max = lax.pmax(jnp.max(unnormalized_log_odds, axis=1), "cent")
         weights_exp = jnp.exp(unnormalized_log_odds - row_max[:, None])
-        row_total = lax.psum(jnp.sum(weights_exp, axis=1), "cent")
+        row_total = jnp.sum(lax.all_gather(jnp.sum(weights_exp, axis=1), "cent"), axis=0)
         resp = weights_exp / row_total[:, None]
         numer = lax.dot_general(
             resp.astype(jnp.bfloat16),

time: 1400 us -> 1220 us (0.87)
  blocking collectives: 562 us -> 404 us
  waiting for transfers between devices: 525 us -> 507 us
    psum x2 -> x0, blocking collectives: 276 us -> none  [on_device(): row_total = lax.psum(jnp.sum(weights_exp, axis=1), 'cent')]
    all_gather x0 -> x2, blocking collectives: none -> 118 us  [on_device(): lax.all_gather(jnp.sum(weights_exp, axis=1), 'cent')]
    psum x2, waiting for transfers between devices: 112 us -> 93.9 us  [on_device(): numer, counts = lax.psum((numer, counts), 'dp')]
  transfers between devices with their start and end apart: 7 -> 7, of which waited for: 6 -> 6; matrix products, arithmetic and copies ran while one was open for 16% -> 19% of each run, Pallas kernels for 0% -> 0%
where the time goes in v1:
time: 1220 us; the launch traced here: 1200 us
  waiting for transfers between devices  507 us (42%)
  blocking collectives  404 us (33%)
  local copies, waits for them, and re-layouts  214 us (18%)
  matrix products  29.1 us (2%)
  other arithmetic  22.4 us (2%)
  between operations  14.3 us (1%)
    all_gather x3, waiting for transfers between devices, merged(): pieces = jax.tree.map(lambda part: lax.all_gather(part, axis), value)  303 us
    pmax x2, blocking collectives, on_device(): row_max = lax.pmax(jnp.max(unnormalized_log_odds, axis=1), 'cent')  261 us
    dynamic_slice x510, local copies, waits for them, and re-layouts, merged(): lax.scan(lambda so_far, section: (join(so_far, section), None), head, tail)  205 us
    all_gather x2, blocking collectives, on_device(): lax.all_gather(jnp.sum(weights_exp, axis=1), 'cent')  118 us
    all_gather x1, waiting for transfers between devices, on_device(): lax.all_gather(queries, ('dp', 'cent'), axis=0, tiled=True)  109 us
    psum x2, waiting for transfers between devices, on_device(): numer, counts = lax.psum((numer, counts), 'dp')  93.9 us
    psum x2, blocking collectives, on_device(): numer, counts = lax.psum((numer, counts), 'dp')  24.9 us
  transfers between devices with their start and end apart: 7, of which 6 were waited for; matrix products, arithmetic and copies ran while one was open for 19% of the time, Pallas kernels for 0%

profile of v1, /device:TPU:2, one launch (start us, length us, event | category | flops | bytes accessed | tf_op | source)
XLA Modules:
  0.0 1201.4 jit_solution(10555574900278775062)
XLA Ops:
  8.7 108.5 %all-gather.20.cloned.1.call-done = bf16[256,4,768]{2,1,0:T(4,128)(2,1)} async-done(((bf16[1,4,768]{2,1,0:T(4,128)(2,1)}), bf16[256,4,768]{2,1,0:T(4,128)(2,1)}) %all-gather.20.cloned.1.call-update) | async-done | bytes 1572880 | tf_op jit(solution)/shard_map/all_gather | solution.py:50
  117.2 2.7 reshape.44
  120.0 2.2 select_reduce_fusion.2
  125.8 97.7 %all-gather.14.cloned.1.call-done = f32[262144]{0:T(1024)} async-done(((f32[1024]{0:T(1024)}), f32[262144]{0:T(1024)}) %all-gather.14.cloned.1.call-update) | async-done | bytes 1048592 | tf_op jit(solution)/shard_map/all_gather | solution.py:14
  224.9 103.3 %all-gather.16.cloned.1.call-done = f32[262144]{0:T(1024)} async-done(((f32[1024]{0:T(1024)}), f32[262144]{0:T(1024)}) %all-gather.16.cloned.1.call-update) | async-done | bytes 1048592 | tf_op jit(solution)/shard_map/all_gather | solution.py:14
  330.6 102.2 %all-gather.18.cloned.1.call-done = f32[262144]{0:T(1024)} async-done(((f32[1024]{0:T(1024)}), f32[262144]{0:T(1024)}) %all-gather.18.cloned.1.call-update) | async-done | bytes 1048592 | tf_op jit(solution)/shard_map/all_gather | solution.py:14
  435.2 218.6 %while.14 = (s32[]{:T(128)}, f32[1024]{0:T(1024)S(1)}, f32[1024]{0:T(1024)S(1)}, f32[1024]{0:T(1024)S(1)}, f32[255,1024]{1,0:T(8,128)S(1)}, /*index=5*/f32[255,1024]{1,0:T(8,128)}, f32[255,1024]{1,0:T(8,128)}, s32[]{:T(128)}) while((s32[]{:T(128)}, f32[1024]{0:T(1024)S(1)}, f32[1024]{0:T(1024)S(1)}, f32[1024]{0:T(1024)S(1)}, ...), condition=%wide.region_21.22_spmd, body=%wide.region_20.21_spmd.sunk | while | flops 7170 | bytes 61541 | solution.py:17
  654.5 6.7 fusion.18
  661.1 130.2 %pmax.14 = f32[4096]{0:T(1024)S(1)} all-reduce(f32[4096]{0:T(1024)S(1)} %get-tuple-element.66), channel_id=1, replica_groups=mesh['dp'=8,'cent'=32] {'cent'}, use_global_device_ids=true, to_apply=%region_2.0 | all-reduce | flops 4096 | bytes 32768 | tf_op jit(solution)/shard_map/pmax | solution.py:37
  791.4 2.8 fusion.5
  794.1 58.7 %all-gather = f32[131072]{0:T(1024)S(1)} all-gather(f32[4096]{0:T(1024)S(1)} %fusion.5), channel_id=2, replica_groups=mesh['dp'=8,'cent'=32] {'cent'}, dimensions={0}, use_global_device_ids=true | all-gather | bytes 540672 | tf_op jit(solution)/shard_map/all_gather | solution.py:39
  853.0 6.8 fusion.10
  859.9 3.0 fusion.14
  862.9 12.4 %psum.29 = f32[256]{0:T(256)S(1)} all-reduce(f32[256]{0:T(256)S(1)} %fusion.14), channel_id=1, replica_groups=mesh['dp'=8,'cent'=32] {'dp'}, use_global_device_ids=true, to_apply=%region_7.0 | all-reduce | flops 256 | bytes 2048 | tf_op jit(solution)/shard_map/psum | solution.py:48
  875.3 48.1 %all-reduce.3.cloned.1.call-done = f32[256,768]{1,0:T(8,128)} async-done(((f32[256,768]{1,0:T(8,128)}), f32[256,768]{1,0:T(8,128)}) %all-reduce.3.cloned.1.call-update) | async-done | bytes 786448 | tf_op jit(solution)/shard_map/psum | solution.py:48
  924.8 6.7 fusion.19
  931.5 131.0 %pmax.15 = f32[4096]{0:T(1024)S(1)} all-reduce(f32[4096]{0:T(1024)S(1)} %get-tuple-element.68), channel_id=1, replica_groups=mesh['dp'=8,'cent'=32] {'cent'}, use_global_device_ids=true, to_apply=%region_10.0 | all-reduce | flops 4096 | bytes 32768 | tf_op jit(solution)/shard_map/pmax | solution.py:37
  1062.5 2.8 fusion.6
  1065.3 58.9 %all-gather.1 = f32[131072]{0:T(1024)S(1)} all-gather(f32[4096]{0:T(1024)S(1)} %fusion.6), channel_id=3, replica_groups=mesh['dp'=8,'cent'=32] {'cent'}, dimensions={0}, use_global_device_ids=true | all-gather | bytes 540672 | tf_op jit(solution)/shard_map/all_gather | solution.py:39
  1124.4 6.8 fusion.8
  1131.2 3.0 fusion.12
  1134.2 12.4 %psum.31 = f32[256]{0:T(256)S(1)} all-reduce(f32[256]{0:T(256)S(1)} %fusion.12), channel_id=1, replica_groups=mesh['dp'=8,'cent'=32] {'dp'}, use_global_device_ids=true, to_apply=%region_15.0 | all-reduce | flops 256 | bytes 2048 | tf_op jit(solution)/shard_map/psum | solution.py:48
  1146.6 45.8 %all-reduce.5.cloned.1.call-done = f32[256,768]{1,0:T(8,128)} async-done(((f32[256,768]{1,0:T(8,128)}), f32[256,768]{1,0:T(8,128)}) %all-reduce.5.cloned.1.call-update) | async-done | bytes 786448 | tf_op jit(solution)/shard_map/psum | solution.py:48
  1192.4 2.1 add_divide_fusion
  (1065 shorter events, 222.4 us)
Async XLA Ops:
  7.2 115.8 %copy-start.1 = (s32[1024]{0:T(1024)S(1)}, s32[1024]{0:T(1024)}, u32[]{:S(2)}) copy-start(s32[1024]{0:T(1024)} %param.11) | copy-start | bytes 12292
  7.2 118.5 %copy-start = (f32[256,768]{1,0:T(8,128)S(1)}, f32[256,768]{1,0:T(8,128)}, u32[]{:S(2)}) copy-start(f32[256,768]{1,0:T(8,128)} %param.9) | copy-start | bytes 2359300
  7.2 110.0 %all-gather.20.cloned.1.call-start = ((), (), s32[]{:S(2)}) async-start(), calls=%async_computation.6 | async-start | bytes 1579008 | tf_op jit(solution)/shard_map/all_gather | solution.py:50
  7.9 215.5 %all-gather.14.cloned.1.call-start = ((), (), s32[]{:S(2)}) async-start(), calls=%async_computation.3 | async-start | bytes 1052672 | tf_op jit(solution)/shard_map/all_gather | solution.py:14
  122.2 206.0 %all-gather.16.cloned.1.call-start = ((), (), s32[]{:S(2)}) async-start(), calls=%async_computation.4 | async-start | bytes 1052672 | tf_op jit(solution)/shard_map/all_gather | solution.py:14
  124.4 308.4 %all-gather.18.cloned.1.call-start = ((), (), s32[]{:S(2)}) async-start(), calls=%async_computation.5 | async-start | bytes 1052672 | tf_op jit(solution)/shard_map/all_gather | solution.py:14
  125.0 529.4 %all-gather.12.cloned.1.call-start = ((), (), s32[]{:S(2)}) async-start(), calls=%async_computation | async-start | bytes 6488064 | tf_op jit(solution)/shard_map/all_gather | solution.py:28
  125.6 797.8 %all-reduce.3.cloned.1.call-start = ((), (), s32[]{:S(2)}) async-start(), calls=%async_computation.1 | async-start | bytes 1572864 | tf_op jit(solution)/shard_map/psum | solution.py:48
  224.9 210.3 %slice-start = ((f32[262144]{0:T(1024)}), f32[1024]{0:T(1024)S(1)}, s32[]{:S(2)}) async-start(f32[262144]{0:T(1024)} %all-gather.14.cloned.1.call-done), calls=%async_computation.7 | async-start | bytes 8192 | tf_op jit(solution)/shard_map/slice | solution.py:15
  328.2 107.0 %slice-start.1 = ((f32[262144]{0:T(1024)}), f32[1024]{0:T(1024)S(1)}, s32[]{:S(2)}) async-start(f32[262144]{0:T(1024)} %all-gather.16.cloned.1.call-done), calls=%async_computation.8 | async-start | bytes 8192 | tf_op jit(solution)/shard_map/slice | solution.py:15
  432.8 2.4 slice-start.2
  859.9 332.5 %all-reduce.5.cloned.1.call-start = ((), (), s32[]{:S(2)}) async-start(), calls=%async_computation.2 | async-start | bytes 1572864 | tf_op jit(solution)/shard_map/psum | solution.py:48
Sparse Core Ops, SparseCore 0:
  11.6 105.6 all-gather.19
  122.3 101.0 all-gather.13
  227.2 100.9 all-gather.15
  331.8 100.9 all-gather.17
  435.2 86.4 all-gather.11
  860.0 63.3 all-reduce.2
  1131.3 61.0 all-reduce.4
